TPU v7x, 32 devices: a whole 2x2x4 slice. The times are simulated.
32 devices in a mesh: run: 8 (over z, y), rep: 4 (over x, core).
Axes of the slice: x: 2, y: 2, z: 4, core: 2. Of those that a mesh axis runs over, the one named last changes fastest.
Arguments:
- edge_feats: bfloat16 [4, 16384, 1280], P('rep', 'run'), may hold values from -6 to 6
- edge_grads: bfloat16 [4, 16384, 640], P('rep', 'run'), may hold values from -0.059814453 to 0.059814453
- edge_system: int32 [4, 16384], P('rep', 'run'), may hold values from 0 to 5, as said below
- edge_count: int32 [4, 8], P('rep', 'run'), may hold values from 1025 to 2048
- coef: float32 [4, 6, 32], P('rep'), may hold values from 0.05 to 1
- weights: float32 [32, 1280, 640], P('rep', 'run'), may hold values from -0.15625 to 0.15625
- first_moment: float32 [32, 1280, 640], P('rep', 'run'), may hold values from -6 to 6
- second_moment: float32 [32, 1280, 640], P('rep', 'run'), may hold values from 1 to 10
Outputs:
- new_weights: float32 [32, 1280, 640], P('rep', 'run')
- new_first: float32 [32, 1280, 640], P('rep', 'run')
- new_second: float32 [32, 1280, 640], P('rep', 'run')
- merged_next: bfloat16 [4, 6, 1280, 640], P('rep', None, 'run')
Inputs may be any that keep to these rules, and one draw needn't show every extreme that they name: `edge_system`: along each replica's rows the system never falls; every system number appears; the live rows of one device belong to one or two systems, two on some device in every draw.
All inputs are finite; a program needn't handle non-finite values.
Results may differ from a plain program's by a relative error of at most 0.001.
The roundings to bfloat16 on the way count: a program that leaves them out, or rounds other values in their place, can miss the bound.
Values may be sent and summed in bfloat16 or wider, within the bound.
A program may use at most 128 MiB of HBM per device.

v0:
```python
import jax
import jax.numpy as jnp
from jax import lax
from jax.sharding import PartitionSpec as P


def on_device(
    edge_feats, edge_grads, edge_system, edge_count, coef, weights, first_moment, second_moment
):
    feats = edge_feats[0]
    grads = edge_grads[0]
    system = edge_system[0]
    live_count = edge_count[0, 0]
    group_coef = coef[0]
    nsys = group_coef.shape[0]
    rows = system.shape[0]
    live = jnp.arange(rows) < live_count
    first = system[0]
    last = lax.dynamic_index_in_dim(system, live_count - 1, 0, keepdims=False)
    has_upper = last > first
    empty = jnp.zeros_like(grads)

    def slot_grad(offset):
        keep = live & (system == first + offset)
        right = jnp.where(keep[:, None], grads, empty)
        return lax.dot_general(
            feats, right, (((0,), (0,)), ((), ())), preferred_element_type=jnp.float32
        )

    lower = slot_grad(0)
    upper = lax.cond(has_upper, lambda: slot_grad(1), lambda: jnp.zeros_like(lower))
    stacked = jnp.stack([lower, upper])
    pieces = lax.all_to_all(stacked, "run", split_axis=1, concat_axis=0, tiled=True)
    high_index = jnp.minimum(first + 1, nsys - 1)
    slot_coef = jnp.stack(
        [group_coef[first], group_coef[high_index] * has_upper.astype(jnp.float32)]
    )
    all_coef = lax.all_gather(slot_coef, "run", axis=0, tiled=True)
    mixed = jnp.einsum("ke,kio->eio", all_coef, pieces, precision=lax.Precision.HIGHEST)
    expert_grad = lax.psum_scatter(mixed, "rep", scatter_dimension=0, tiled=True)
    new_first = 0.9 * first_moment + 0.1 * expert_grad
    new_second = 0.999 * second_moment + 0.001 * expert_grad * expert_grad
    corr_first = 1.0 - 0.9**10
    corr_second = 1.0 - 0.999**10
    new_weights = weights - 0.01 * (new_first / corr_first) / (
        jnp.sqrt(new_second / corr_second) + 1e-08
    )
    rounded = lax.optimization_barrier(new_weights.astype(jnp.bfloat16))
    every_expert = lax.all_gather(rounded, "rep", axis=0, tiled=True)
    experts, din_local, dout = every_expert.shape
    flat = every_expert.astype(jnp.float32).reshape(experts, din_local * dout)
    merged = jnp.dot(group_coef, flat, precision=lax.Precision.HIGHEST)
    merged_next = merged.reshape(nsys, din_local, dout).astype(jnp.bfloat16)
    return (new_weights, new_first, new_second, merged_next[None])


def solution(mesh):
    placed = (
        P("rep", "run", None),
        P("rep", "run", None),
        P("rep", "run"),
        P("rep", "run"),
        P("rep", None, None),
        P("rep", "run", None),
        P("rep", "run", None),
        P("rep", "run", None),
    )
    return jax.shard_map(
        on_device,
        mesh=mesh,
        in_specs=placed,
        out_specs=(
            P("rep", "run", None),
            P("rep", "run", None),
            P("rep", "run", None),
            P("rep", None, "run", None),
        ),
        check_vma=False,
    )
```

profile of v0, /device:TPU:0, one launch (start us, length us, event | category | flops | bytes accessed | tf_op | source)
XLA Modules:
  0.0 418.8 jit_solution(7868111956152384483)
XLA Ops:
  7.8 1.3 constant_dynamic-slice_fusion
  9.1 1.4 compare_reduce_fusion.1
  11.8 0.0 copy-start.1
  11.8 8.7 %convolution_bitcast_fusion.1 = f32[1,1280,640]{1,2,0:T(8,128)} fusion(bf16[1,2048,640]{2,1,0:T(8,128)(2,1)} %param.11, pred[2048]{0:T(1024)(128)(4,1)S(1)} %fusion.9, bf16[1,2048,1280]{2,1,0:T(8,128)(2,1)} %param.10), kind=kOutput, calls=%fused_computation.10 | convolution fusion | flops 3356753920 | bytes 11143168 | tf_op jit(solution)/shard_map/dot_general | solution.py:26
  20.5 0.0 copy-done.1
  20.5 0.2 conditional.1
  20.5 0.2 stack.12
  20.8 5.1 %pad_maximum_fusion = f32[2,1280,640]{1,2,0:T(8,128)} fusion(f32[1,1280,640]{1,2,0:T(8,128)S(1)} %get-tuple-element.50, f32[1,1280,640]{1,2,0:T(8,128)} %convolution_bitcast_fusion.1), kind=kLoop, calls=%fused_computation.8 | loop fusion | flops 1638400 | bytes 13107200 | tf_op jit(solution)/shard_map/stack | solution.py:32
  25.8 11.9 %copy.29 = f32[2,1280,640]{2,0,1:T(2,128)} copy(f32[2,1280,640]{1,2,0:T(8,128)} %pad_maximum_fusion) | data formatting | bytes 13107200 | tf_op jit(solution)/shard_map/stack | solution.py:32
  37.8 0.0 copy-start.2
  37.8 15.6 %all-to-all-start = ((f32[2,1280,640]{2,0,1:T(2,128)}), f32[2,1280,640]{2,0,1:T(2,128)}, u32[]{:S(2)}, u32[]{:S(2)}) async-start(f32[2,1280,640]{2,0,1:T(2,128)} %copy.29), calls=%async_computation | async-start | bytes 13107200 | tf_op jit(solution)/shard_map/all_to_all | solution.py:33
  53.4 0.0 reduce-scatter.2.cloned.1.call-start
  56.0 0.0 copy-done.2
  56.1 118.6 %all-gather = f32[8,2,32]{2,1,0:T(2,128)S(1)} all-gather(f32[1,2,32]{2,1,0:T(2,128)S(1)} %maximum_bitcast_fusion), channel_id=1, replica_groups=mesh['run'=8,'rep'=4] {'run'}, dimensions={0}, use_global_device_ids=true | all-gather | bytes 2304 | tf_op jit(solution)/shard_map/all_gather | solution.py:38
  174.7 22.6 %all-to-all-done = f32[2,1280,640]{2,0,1:T(2,128)} async-done(((f32[2,1280,640]{2,0,1:T(2,128)}), f32[2,1280,640]{2,0,1:T(2,128)}, u32[]{:S(2)}, u32[]{:S(2)}) %all-to-all-start) | async-done | bytes 6553632 | tf_op jit(solution)/shard_map/all_to_all | solution.py:33
  197.3 6.0 %copy.30 = f32[2,1280,640]{2,1,0:T(8,128)} copy(f32[2,1280,640]{2,0,1:T(2,128)} %all-to-all-done) | data formatting | bytes 13107200 | tf_op jit(solution)/shard_map/all_to_all | solution.py:33
  203.3 10.6 %copy.31 = f32[8,2,160,640]{3,1,0,2:T(2,128)} copy(f32[8,2,160,640]{3,2,0,1:T(8,128)} %bitcast.53) | data formatting | bytes 13107200 | tf_op jit(solution)/shard_map/all_to_all | solution.py:33
  213.9 8.6 %all_to_all.16 = f32[16,160,640]{2,0,1:T(8,128)} reshape(f32[8,2,160,640]{3,1,0,2:T(2,128)} %copy.31) | data formatting | bytes 13107200 | tf_op jit(solution)/shard_map/all_to_all | solution.py:33
  222.5 14.2 %fusion.20 = f32[32,160,640]{2,0,1:T(8,128)} fusion(f32[16,32,1]{1,0,2:T(8,128)S(1)} %bitcast.56, f32[16,160,640]{2,0,1:T(8,128)} %all_to_all.16), kind=kOutput, calls=%fused_computation.36 | convolution fusion | flops 629145600 | bytes 19662848 | tf_op jit(solution)/shard_map/ke,kio->eio/dot_general | solution.py:39
  236.8 0.0 reduce-scatter.2.cloned.1.call-update
  236.8 0.3 all-gather.3.cloned.1.call-start
  237.1 107.3 %reduce-scatter.2.cloned.1.call-done = f32[8,160,640]{2,0,1:T(8,128)} async-done(((f32[32,160,640]{2,0,1:T(8,128)}), f32[8,160,640]{2,0,1:T(8,128)}) %reduce-scatter.2.cloned.1.call-update) | async-done | bytes 3276816 | tf_op jit(solution)/shard_map/reduce_scatter | solution.py:40
  344.4 12.3 %fusion.17 = (bf16[8,160,640]{2,0,1:T(8,128)(2,1)}, f32[8,160,640]{2,0,1:T(8,128)}, f32[8,160,640]{2,0,1:T(8,128)}, f32[8,160,640]{2,0,1:T(8,128)S(1)}) fusion(f32[8,160,640]{2,1,0:T(8,128)} %param.15, f32[8,160,640]{2,0,1:T(8,128)} %reduce-scatter.2.cloned.1.call-done, f32[8,160,640]{2,1,0:T(8,128)} %param.16, f32[8,160,640]{2,1,0:T(8,128)} %param.17), kind=kLoop, calls=%fused_computation.35 | loop fusion | flops 10649600 | bytes 24576000 | tf_op jit(solution)/shard_map/convert_element_type | solution.py:48
  356.7 0.0 all-gather.3.cloned.1.call-update
  356.8 0.0 copy-start
  356.8 4.4 %copy.35 = f32[8,160,640]{2,1,0:T(8,128)} copy(f32[8,160,640]{2,0,1:T(8,128)} %get-tuple-element.43) | data formatting | bytes 6553600
  361.2 0.0 copy-done
  361.2 2.3 copy.36
  363.5 2.3 copy.37
  365.8 38.9 %all-gather.3.cloned.1.call-done = bf16[32,160,640]{2,0,1:T(8,128)(2,1)} async-done(((bf16[8,160,640]{2,0,1:T(8,128)(2,1)}), bf16[32,160,640]{2,0,1:T(8,128)(2,1)}) %all-gather.3.cloned.1.call-update) | async-done | bytes 6553616 | tf_op jit(solution)/shard_map/all_gather | solution.py:49
  404.7 3.4 copy.39
  408.2 2.7 convolution_convert_fusion
  410.8 1.2 copy.56
  (4 shorter events, 0.0 us)
Async XLA Ops:
  11.8 8.8 %copy-start.1 = (s32[1,2048]{1,0:T(1,128)S(1)}, s32[1,2048]{1,0:T(1,128)}, u32[]{:S(2)}) copy-start(s32[1,2048]{1,0:T(1,128)} %param.12) | copy-start | bytes 24580
  37.8 18.3 %copy-start.2 = (f32[1,6,32]{2,0,1:T(1,128)S(1)}, f32[1,6,32]{2,0,1:T(1,128)}, u32[]{:S(2)}) copy-start(f32[1,6,32]{2,0,1:T(1,128)} %param.14) | copy-start | bytes 2308
  37.8 159.5 %all-to-all-start = ((f32[2,1280,640]{2,0,1:T(2,128)}), f32[2,1280,640]{2,0,1:T(2,128)}, u32[]{:S(2)}, u32[]{:S(2)}) async-start(f32[2,1280,640]{2,0,1:T(2,128)} %copy.29), calls=%async_computation | async-start | bytes 13107200 | tf_op jit(solution)/shard_map/all_to_all | solution.py:33
  53.4 291.0 %reduce-scatter.2.cloned.1.call-start = ((), (), s32[]{:S(2)}) async-start(), calls=%async_computation.2 | async-start | bytes 16384000 | tf_op jit(solution)/shard_map/reduce_scatter | solution.py:40
  236.8 167.9 %all-gather.3.cloned.1.call-start = ((), (), s32[]{:S(2)}) async-start(), calls=%async_computation.3 | async-start | bytes 8192000 | tf_op jit(solution)/shard_map/all_gather | solution.py:49
  356.8 4.4 %copy-start = (f32[8,160,640]{2,0,1:T(8,128)S(1)}, f32[8,160,640]{2,0,1:T(8,128)}, u32[]{:S(2)}) copy-start(f32[8,160,640]{2,0,1:T(8,128)} %get-tuple-element.44) | copy-start | bytes 9830404
Sparse Core Ops, SparseCore 0:
  236.9 107.4 reduce-scatter.1
  356.9 47.7 all-gather.2
where the time goes:
time: 420 us; the launch traced here: 419 us
  waiting for transfers between devices  169 us (40%)
  blocking collectives  119 us (28%)
  local copies, waits for them, and re-layouts  52.3 us (12%)
  matrix products  25.6 us (6%)
  other arithmetic  18.8 us (4%)
  between operations  18.7 us (4%)
  starting transfers between devices  15.9 us (4%)
    all_gather x1, blocking collectives, on_device(): all_coef = lax.all_gather(slot_coef, 'run', axis=0, tiled=True)  119 us
    reduce_scatter x1, waiting for transfers between devices, on_device(): lax.psum_scatter(mixed, 'rep', scatter_dimension=0, tiled=True)  107 us
    all_gather x1, waiting for transfers between devices, on_device(): every_expert = lax.all_gather(rounded, 'rep', axis=0, tiled=True)  38.9 us
    all_to_all x3, local copies, waits for them, and re-layouts, on_device(): lax.all_to_all(stacked, 'run', split_axis=1, concat_axis=0, tiled=True)  25.3 us
    all_to_all x1, waiting for transfers between devices, on_device(): lax.all_to_all(stacked, 'run', split_axis=1, concat_axis=0, tiled=True)  22.6 us
    all_to_all x1, starting transfers between devices, on_device(): lax.all_to_all(stacked, 'run', split_axis=1, concat_axis=0, tiled=True)  15.6 us
    dot_general x1, matrix products, on_device(): jnp.einsum('ke,kio->eio', all_coef, pieces, precision=lax.Precision.HIGHEST)  14.2 us
    convert_element_type x1, other arithmetic, on_device(): rounded = lax.optimization_barrier(new_weights.astype(jnp.bfloat16))  12.3 us
  transfers between devices with their start and end apart: 3, of which 3 were waited for; matrix products, arithmetic and copies ran while one was open for 2% of the time, Pallas kernels for 0%

commit v1 on v0

--- a/solution.py
+++ b/solution.py
@@ -30,7 +30,13 @@
     lower = slot_grad(0)
     upper = lax.cond(has_upper, lambda: slot_grad(1), lambda: jnp.zeros_like(lower))
     stacked = jnp.stack([lower, upper])
-    pieces = lax.all_to_all(stacked, "run", split_axis=1, concat_axis=0, tiled=True)
+    order_lane = lambda inp, chip_axis, array_axis, array_dim: jnp.concatenate(
+        lax.all_to_all(
+            jnp.stack(jnp.split(inp, lax.axis_size(chip_axis), axis=array_axis)), chip_axis, 0, 0
+        ),
+        axis=array_dim,
+    )
+    pieces = order_lane(stacked, "run", 1, 0)
     high_index = jnp.minimum(first + 1, nsys - 1)
     slot_coef = jnp.stack(
         [group_coef[first], group_coef[high_index] * has_upper.astype(jnp.float32)]

time: 420 us -> 401 us (0.955)
  local copies, waits for them, and re-layouts: 52.3 us -> 25.1 us
  other arithmetic: 18.8 us -> 26.2 us
    all_to_all x3 -> x0, local copies, waits for them, and re-layouts: 25.3 us -> none  [on_device(): lax.all_to_all(stacked, 'run', split_axis=1, concat_axis=0, tiled=True)]
    another operation x2 -> x1, local copies, waits for them, and re-layouts: 12.2 us -> 0.21 us  [on_device(): stacked = jnp.stack([lower, upper])]
    unnamed x1 -> x8, other arithmetic: 0.01 us -> 11 us
    another operation x0 -> x1, local copies, waits for them, and re-layouts: none -> 10 us  [on_device(): jnp.stack(jnp.split(inp, lax.axis_size(chip_axis), axis=array_axis))]
    unnamed x10 -> x12, local copies, waits for them, and re-layouts: 10.2 us -> 10.2 us
where the time goes in v1:
time: 401 us; the launch traced here: 400 us
  waiting for transfers between devices  169 us (42%)
  blocking collectives  119 us (30%)
  matrix products  26.6 us (7%)
  other arithmetic  26.2 us (7%)
  local copies, waits for them, and re-layouts  25.1 us (6%)
  between operations  18.7 us (5%)
  starting transfers between devices  15.7 us (4%)
    all_gather x1, blocking collectives, on_device(): all_coef = lax.all_gather(slot_coef, 'run', axis=0, tiled=True)  119 us
    reduce_scatter x1, waiting for transfers between devices, on_device(): lax.psum_scatter(mixed, 'rep', scatter_dimension=0, tiled=True)  108 us
    all_gather x1, waiting for transfers between devices, on_device(): every_expert = lax.all_gather(rounded, 'rep', axis=0, tiled=True)  38.9 us
    all_to_all x1, waiting for transfers between devices, on_device(): lax.all_to_all(jnp.stack(jnp.split(inp, lax.axis_size(chip_axis), axis=ar...  22.6 us
    all_to_all x1, starting transfers between devices, on_device(): lax.all_to_all(jnp.stack(jnp.split(inp, lax.axis_size(chip_axis), axis=ar...  15.6 us
    dot_general x1, matrix products, on_device(): jnp.einsum('ke,kio->eio', all_coef, pieces, precision=lax.Precision.HIGHEST)  15.2 us
    convert_element_type x1, other arithmetic, on_device(): rounded = lax.optimization_barrier(new_weights.astype(jnp.bfloat16))  12.3 us
    unnamed x8, other arithmetic  11 us
  transfers between devices with their start and end apart: 3, of which 3 were waited for; matrix products, arithmetic and copies ran while one was open for 2% of the time, Pallas kernels for 0%

profile of v1, /device:TPU:0, one launch (start us, length us, event | category | flops | bytes accessed | tf_op | source)
XLA Modules:
  0.0 399.9 jit_solution(4693919392894131651)
XLA Ops:
  7.8 1.3 constant_dynamic-slice_fusion
  9.1 1.4 compare_reduce_fusion.1
  11.8 0.0 copy-start.2
  11.8 8.7 %convolution_bitcast_fusion.1 = f32[1,1280,640]{1,2,0:T(8,128)} fusion(bf16[1,2048,640]{2,1,0:T(8,128)(2,1)} %param.11, pred[2048]{0:T(1024)(128)(4,1)S(1)} %fusion.34, bf16[1,2048,1280]{2,1,0:T(8,128)(2,1)} %param.10), kind=kOutput, calls=%fused_computation.25 | convolution fusion | flops 3356753920 | bytes 11143168 | tf_op jit(solution)/shard_map/dot_general | solution.py:26
  20.5 0.0 copy-done.2
  20.5 0.2 conditional.1
  20.5 0.2 stack.30
  20.8 0.0 copy-start
  20.8 2.4 fusion.15
  23.2 0.0 copy-done
  23.2 1.5 fusion.18
  24.6 1.5 fusion.21
  26.1 1.5 fusion.24
  27.6 1.2 fusion.27
  28.7 1.5 fusion.30
  30.2 1.5 fusion.12
  31.8 1.4 fusion.32
  33.2 10.0 %copy.28 = f32[8,2,160,640]{3,2,1,0:T(8,128)} copy(f32[8,2,160,640]{2,3,1,0:T(8,128)} %fusion.32) | data formatting | bytes 13107200 | tf_op jit(solution)/shard_map/stack | solution.py:35
  43.2 0.0 copy-start.3
  43.2 15.6 %all-to-all-start = ((f32[8,2,160,640]{3,2,1,0:T(8,128)}), f32[8,2,160,640]{3,2,1,0:T(8,128)}, u32[]{:S(2)}, u32[]{:S(2)}) async-start(f32[8,2,160,640]{3,2,1,0:T(8,128)} %copy.28), calls=%async_computation | async-start | bytes 13107200 | tf_op jit(solution)/shard_map/all_to_all | solution.py:34
  58.8 0.0 reduce-scatter.2.cloned.1.call-start
  61.5 0.0 copy-done.3
  61.5 118.6 %all-gather = f32[8,2,32]{2,1,0:T(2,128)S(1)} all-gather(f32[1,2,32]{2,1,0:T(2,128)S(1)} %maximum_bitcast_fusion), channel_id=1, replica_groups=mesh['run'=8,'rep'=4] {'run'}, dimensions={0}, use_global_device_ids=true | all-gather | bytes 2304 | tf_op jit(solution)/shard_map/all_gather | solution.py:44
  180.1 22.6 %all-to-all-done = f32[8,2,160,640]{3,2,1,0:T(8,128)} async-done(((f32[8,2,160,640]{3,2,1,0:T(8,128)}), f32[8,2,160,640]{3,2,1,0:T(8,128)}, u32[]{:S(2)}, u32[]{:S(2)}) %all-to-all-start) | async-done | bytes 6553632 | tf_op jit(solution)/shard_map/all_to_all | solution.py:34
  202.7 15.2 %fusion.3 = f32[32,160,640]{2,0,1:T(8,128)} fusion(f32[16,32,1]{1,0,2:T(8,128)S(1)} %bitcast.82, f32[16,160,640]{2,1,0:T(8,128)} %bitcast.23), kind=kOutput, calls=%fused_computation.22 | convolution fusion | flops 629145600 | bytes 19662848 | tf_op jit(solution)/shard_map/ke,kio->eio/dot_general | solution.py:45
  217.9 0.0 reduce-scatter.2.cloned.1.call-update
  217.9 0.0 all-gather.3.cloned.1.call-start
  217.9 107.6 %reduce-scatter.2.cloned.1.call-done = f32[8,160,640]{2,0,1:T(8,128)} async-done(((f32[32,160,640]{2,0,1:T(8,128)}), f32[8,160,640]{2,0,1:T(8,128)}) %reduce-scatter.2.cloned.1.call-update) | async-done | bytes 3276816 | tf_op jit(solution)/shard_map/reduce_scatter | solution.py:46
  325.5 12.3 %fusion.42 = (bf16[8,160,640]{2,0,1:T(8,128)(2,1)}, f32[8,160,640]{2,0,1:T(8,128)}, f32[8,160,640]{2,0,1:T(8,128)}, f32[8,160,640]{2,0,1:T(8,128)S(1)}) fusion(f32[8,160,640]{2,1,0:T(8,128)} %param.15, f32[8,160,640]{2,0,1:T(8,128)} %reduce-scatter.2.cloned.1.call-done, f32[8,160,640]{2,1,0:T(8,128)} %param.16, f32[8,160,640]{2,1,0:T(8,128)} %param.17), kind=kLoop, calls=%fused_computation.74 | loop fusion | flops 10649600 | bytes 24576000 | tf_op jit(solution)/shard_map/convert_element_type | solution.py:54
  337.8 0.0 all-gather.3.cloned.1.call-update
  337.9 0.0 copy-start.1
  337.9 4.4 %copy.33 = f32[8,160,640]{2,1,0:T(8,128)} copy(f32[8,160,640]{2,0,1:T(8,128)} %get-tuple-element.43) | data formatting | bytes 6553600
  342.3 0.0 copy-done.1
  342.3 2.3 copy.34
  344.6 2.3 copy.35
  346.9 38.9 %all-gather.3.cloned.1.call-done = bf16[32,160,640]{2,0,1:T(8,128)(2,1)} async-done(((bf16[8,160,640]{2,0,1:T(8,128)(2,1)}), bf16[32,160,640]{2,0,1:T(8,128)(2,1)}) %all-gather.3.cloned.1.call-update) | async-done | bytes 6553616 | tf_op jit(solution)/shard_map/all_gather | solution.py:55
  385.8 3.4 copy.38
  389.2 2.7 convolution_convert_fusion
  391.9 1.2 copy.57
  (4 shorter events, 0.0 us)
Async XLA Ops:
  11.8 8.8 %copy-start.2 = (s32[1,2048]{1,0:T(1,128)S(1)}, s32[1,2048]{1,0:T(1,128)}, u32[]{:S(2)}) copy-start(s32[1,2048]{1,0:T(1,128)} %param.12) | copy-start | bytes 24580
  20.8 2.4 copy-start
  43.2 18.3 %copy-start.3 = (f32[1,6,32]{2,0,1:T(1,128)S(1)}, f32[1,6,32]{2,0,1:T(1,128)}, u32[]{:S(2)}) copy-start(f32[1,6,32]{2,0,1:T(1,128)} %param.14) | copy-start | bytes 2308
  43.2 159.5 %all-to-all-start = ((f32[8,2,160,640]{3,2,1,0:T(8,128)}), f32[8,2,160,640]{3,2,1,0:T(8,128)}, u32[]{:S(2)}, u32[]{:S(2)}) async-start(f32[8,2,160,640]{3,2,1,0:T(8,128)} %copy.28), calls=%async_computation | async-start | bytes 13107200 | tf_op jit(solution)/shard_map/all_to_all | solution.py:34
  58.8 266.6 %reduce-scatter.2.cloned.1.call-start = ((), (), s32[]{:S(2)}) async-start(), calls=%async_computation.2 | async-start | bytes 16384000 | tf_op jit(solution)/shard_map/reduce_scatter | solution.py:46
  217.9 167.9 %all-gather.3.cloned.1.call-start = ((), (), s32[]{:S(2)}) async-start(), calls=%async_computation.3 | async-start | bytes 8192000 | tf_op jit(solution)/shard_map/all_gather | solution.py:55
  337.9 4.4 %copy-start.1 = (f32[8,160,640]{2,0,1:T(8,128)S(1)}, f32[8,160,640]{2,0,1:T(8,128)}, u32[]{:S(2)}) copy-start(f32[8,160,640]{2,0,1:T(8,128)} %get-tuple-element.44) | copy-start | bytes 9830404
Sparse Core Ops, SparseCore 0:
  218.0 107.4 reduce-scatter.1
  338.0 47.7 all-gather.2
